TPU v7x, 128 devices: a whole 4x4x4 slice. The times are simulated.
128 devices in a mesh: dp: 8 (over z, core), tensor: 16 (over x, y).
Axes of the slice: x: 4, y: 4, z: 4, core: 2. Of those that a mesh axis runs over, the one named last changes fastest.
Arguments:
- residual_in: bfloat16 [1024, 4096], P('dp'), may hold values from -3 to 3
- query: bfloat16 [1024, 8192], P('dp', 'tensor'), may hold values from -130 to 130
- fresh_key: bfloat16 [1024, 4, 128], P('dp'), may hold values from -5 to 5
- fresh_value: bfloat16 [1024, 4, 128], P('dp'), may hold values from -10 to 10
- key_cache: bfloat16 [1024, 16, 128, 128], P('dp', 'tensor'), may hold values from -5 to 5, as said below
- value_cache: bfloat16 [1024, 16, 128, 128], P('dp', 'tensor'), may hold values from -10 to 10, as said below
- lengths: int32 [1024], P('dp'), may hold values from 2 to 128
- out_weight: bfloat16 [8192, 4096], P('tensor'), may hold values from -0.0625 to 0.0625
- norm_gain: float32 [4096], replicated, may hold values from 0.1 to 1.9
- expert_ids: int32 [1024, 8], P('dp'), may hold values from 0 to 127, all different within a row; in each aligned block of 128 rows (0 to 127, 128 to 255, ...) at most 16 rows name the same one
- gate_scores: float32 [1024, 8], P('dp'), may hold values from 0.05 to 1
- w_gate: bfloat16 [128, 4096, 768], P(('dp', 'tensor')), may hold values from -0.09375 to 0.09375
- w_up: bfloat16 [128, 4096, 768], P(('dp', 'tensor')), may hold values from -0.09375 to 0.09375
- w_down: bfloat16 [128, 768, 4096], P(('dp', 'tensor')), may hold values from -0.21875 to 0.21875
Outputs:
- layer_out: bfloat16 [1024, 4096], P(('dp', 'tensor'))
Inputs may be any that keep to these rules, and one draw needn't show every extreme that they name: `expert_ids`: each row names 8 different experts; among the 128 rows of one data replica (aligned blocks) no expert is named by more than 16 rows, a bound that some block reaches. `key_cache`: the copies of one key head are equal. `value_cache`: the copies of one value head are equal.
All inputs are finite; a program needn't handle non-finite values.
Results may differ from a plain program's by a relative error of at most 0.023.
Values may be sent and summed in bfloat16 or wider, within the bound.
No kernel may reach another device: no remote copies, remote signals or barrier semaphores. Data moves between devices by JAX's collectives and lax.ppermute only.
A program may use at most 128 MiB of HBM per device.

v0:
```python
import jax
import jax.numpy as jnp
from jax import lax
from jax.sharding import PartitionSpec as P


def rms_normalize(hidden, norm_gain):
    widened = hidden.astype(jnp.float32)
    spread = jnp.mean(widened * widened, axis=-1, keepdims=True)
    return (widened * lax.rsqrt(spread + 1e-06) * norm_gain).astype(jnp.bfloat16)


def shards(
    residual_in,
    query,
    fresh_key,
    fresh_value,
    key_cache,
    value_cache,
    lengths,
    out_weight,
    norm_gain,
    expert_ids,
    gate_scores,
    w_gate,
    w_up,
    w_down,
):
    row_count = residual_in.shape[0]
    head_size = key_cache.shape[3]
    tensor_width = lax.axis_size("tensor")
    column = lax.axis_index("tensor")
    kv_head = column // (tensor_width // fresh_key.shape[1])
    head_count = query.shape[1] // head_size
    score_scale = head_size ** (-0.5)
    query_rows = query.reshape(row_count, head_count, head_size)
    cached_keys = key_cache[:, 0]
    cached_values = value_cache[:, 0]
    own_key = lax.dynamic_index_in_dim(fresh_key, kv_head, 1, keepdims=False)
    own_value = lax.dynamic_index_in_dim(fresh_value, kv_head, 1, keepdims=False)
    scores = (
        jnp.einsum("rhd,rpd->rhp", query_rows, cached_keys, preferred_element_type=jnp.float32)
        * score_scale
    )
    own_score = (
        jnp.einsum("rhd,rd->rh", query_rows, own_key, preferred_element_type=jnp.float32)
        * score_scale
    )
    in_cache = (
        lax.broadcasted_iota(jnp.int32, (row_count, cached_keys.shape[1]), 1) < lengths[:, None]
    )
    scores = jnp.where(in_cache[:, None, :], scores, -1e30)
    row_max = jnp.maximum(jnp.max(scores, axis=-1), own_score)
    cache_terms = jnp.exp(scores - row_max[..., None])
    own_term = jnp.exp(own_score - row_max)
    denom = jnp.sum(cache_terms, axis=-1) + own_term
    probs = (cache_terms / denom[..., None]).astype(jnp.bfloat16)
    own_prob = (own_term / denom).astype(jnp.bfloat16)
    attended = jnp.einsum("rhp,rpd->rhd", probs, cached_values, preferred_element_type=jnp.float32)
    attended = (
        attended
        + own_prob.astype(jnp.float32)[..., None] * own_value.astype(jnp.float32)[:, None, :]
    )
    heads_out = attended.astype(jnp.bfloat16).reshape(row_count, head_count * head_size)
    share_rows = row_count // tensor_width
    first_own = column * share_rows
    proj = lax.psum(
        jnp.dot(heads_out, out_weight, preferred_element_type=jnp.float32).astype(jnp.bfloat16),
        "tensor",
    ).astype(jnp.float32)
    hidden_all = (residual_in.astype(jnp.float32) + proj).astype(jnp.bfloat16)
    normed = rms_normalize(hidden_all, norm_gain)
    hidden_own = lax.dynamic_slice_in_dim(hidden_all, first_own, share_rows, 0)
    replica_count = lax.axis_size("dp")
    experts_all = replica_count * tensor_width
    topk_count = expert_ids.shape[1]
    cap_slots = 2 * max(1, row_count * topk_count // experts_all)
    targets = lax.broadcasted_iota(jnp.int32, (replica_count,), 0) * tensor_width + column
    matches = expert_ids[:, :, None] == targets[None, None, :]
    weights = gate_scores / jnp.sum(gate_scores, axis=1, keepdims=True)
    routed = jnp.any(matches, axis=1)
    picked_weight = jnp.sum(jnp.where(matches, weights[:, :, None], 0.0), axis=1)
    slot_index = jnp.cumsum(routed.astype(jnp.int32), axis=0) - 1
    slot_ids = lax.broadcasted_iota(jnp.int32, (1, cap_slots, 1), 1)
    selector = ((slot_index.T[:, None, :] == slot_ids) & routed.T[:, None, :]).astype(jnp.bfloat16)
    outgoing = jnp.einsum(
        "bcr,rd->bcd", selector, normed, preferred_element_type=jnp.float32
    ).astype(jnp.bfloat16)
    received = lax.all_to_all(outgoing, "dp", split_axis=0, concat_axis=0, tiled=True)
    flat_rows = received.reshape(-1, received.shape[2])
    gate_part = jnp.dot(flat_rows, w_gate[0], preferred_element_type=jnp.float32)
    up_part = jnp.dot(flat_rows, w_up[0], preferred_element_type=jnp.float32)
    act = (jax.nn.silu(gate_part) * up_part).astype(jnp.bfloat16)
    result = jnp.dot(act, w_down[0], preferred_element_type=jnp.float32).astype(jnp.bfloat16)
    answered = result.reshape(received.shape)
    returned_rows = lax.all_to_all(answered, "dp", split_axis=0, concat_axis=0, tiled=True)
    gathered = jnp.einsum(
        "bcr,bcd->brd", selector, returned_rows, preferred_element_type=jnp.float32
    )
    mixture_own = lax.psum_scatter(
        jnp.sum(picked_weight.T[:, :, None] * gathered, axis=0).astype(jnp.bfloat16),
        "tensor",
        scatter_dimension=0,
        tiled=True,
    ).astype(jnp.float32)
    return (hidden_own.astype(jnp.float32) + mixture_own).astype(jnp.bfloat16)


def solution(mesh):
    placed = (
        P("dp", None),
        P("dp", "tensor"),
        P("dp", None, None),
        P("dp", None, None),
        P("dp", "tensor", None, None),
        P("dp", "tensor", None, None),
        P("dp"),
        P("tensor", None),
        P(),
        P("dp", None),
        P("dp", None),
        P(("dp", "tensor"), None, None),
        P(("dp", "tensor"), None, None),
        P(("dp", "tensor"), None, None),
    )
    return jax.shard_map(
        shards, mesh=mesh, in_specs=placed, out_specs=P(("dp", "tensor"), None), check_vma=False
    )
```

profile of v0, /device:TPU:0, one launch (start us, length us, event | category | flops | bytes accessed | tf_op | source)
XLA Modules:
  0.0 260.0 jit_solution(1109410905941494168)
XLA Ops:
  6.5 1.1 dynamic-slice_convert_fusion
  7.6 0.9 reshape.50
  8.6 0.3 fusion.54
  8.9 0.8 iota_compare_fusion.1
  9.7 4.5 %fusion.65 = (f32[128,4]{1,0:T(8,128)S(1)}, f32[128,4,128]{2,1,0:T(4,128)S(1)}) fusion(bf16[128,4,128]{2,1,0:T(4,128)(2,1)S(1)} %reshape.50, bf16[128,1,128,128]{3,2,1,0:T(8,128)(2,1)} %param.18, pred[128,128]{1,0:T(8,128)(4,1)S(1)} %iota_compare_fusion.1), kind=kOutput, calls=%fused_computation.69 | convolution fusion | flops 16973312 | bytes 4605952 | tf_op jit(solution)/shard_map/rhd,rpd->rhp/dot_general | solution.py:42
  14.3 0.1 copy.40
  14.4 0.4 fusion.45
  14.9 0.1 copy.42
  15.0 0.1 copy.43
  15.2 3.6 %fusion.31 = bf16[128,4,128]{2,1,0:T(4,128)(2,1)S(1)} fusion(bf16[128,1,128,128]{3,2,1,0:T(8,128)(2,1)} %param.19, f32[128,4,128]{2,1,0:T(4,128)S(1)} %get-tuple-element.10, f32[128,128]{1,0:T(8,128)S(1)} %bitcast.77, f32[128,4]{1,0:T(8,128)S(1)} %copy.43, f32[128,4]{1,0:T(8,128)S(1)} %copy.42, f32[128,4]{1,0:T(8,128)S(1)} %copy.40), kind=kOutput, calls=%fused_computation.25 | convolution fusion | flops 17170432 | bytes 4659200 | tf_op jit(solution)/shard_map/rhp,rpd->rhd/dot_general | solution.py:59
  18.8 1.8 convolution_convert_fusion.1
  20.8 0.2 reduce_window_sum.11
  21.0 89.0 %all-reduce.4.cloned.1.call-done = bf16[128,4096]{1,0:T(8,128)(2,1)} async-done(((bf16[128,4096]{1,0:T(8,128)(2,1)}), bf16[128,4096]{1,0:T(8,128)(2,1)}) %all-reduce.4.cloned.1.call-update) | async-done | bytes 1048592 | tf_op jit(solution)/shard_map/psum | solution.py:67
  110.1 1.7 fusion.13
  111.8 0.5 convolution_convert_fusion
  112.3 20.3 %all_to_all.10 = bf16[8,16,4096]{2,1,0:T(8,128)(2,1)S(1)} all-to-all(bf16[8,16,4096]{2,1,0:T(8,128)(2,1)S(1)} %convolution_convert_fusion), channel_id=1, replica_groups=mesh['dp'=8,'tensor'=16] {'dp'}, dimensions={0} | all-to-all | bytes 2097152 | tf_op jit(solution)/shard_map/all_to_all | solution.py:89
  132.6 3.8 %fusion.4 = f32[128,768]{1,0:T(8,128)S(1)} fusion(bf16[128,4096]{1,0:T(8,128)(2,1)S(1)} %bitcast.74, bf16[1,4096,768]{2,1,0:T(8,128)(2,1)} %param.25), kind=kOutput, calls=%fused_computation.5 | convolution fusion | flops 805306368 | bytes 7733248 | tf_op jit(solution)/shard_map/dot_general | solution.py:91
  136.4 8.1 %fusion.6 = bf16[128,4096]{1,0:T(8,128)(2,1)} fusion(bf16[1,768,4096]{2,1,0:T(8,128)(2,1)} %param.27, bf16[128,4096]{1,0:T(8,128)(2,1)S(1)} %bitcast.75, bf16[1,4096,768]{2,1,0:T(8,128)(2,1)} %param.26, f32[128,768]{1,0:T(8,128)S(1)} %fusion.4), kind=kOutput, calls=%fused_computation.7 | convolution fusion | flops 1611726848 | bytes 15073280 | tf_op jit(solution)/shard_map/dot_general | solution.py:94
  144.5 3.6 %all-to-all-start.1 = ((bf16[8,16,4096]{2,1,0:T(8,128)(2,1)}), bf16[8,16,4096]{2,1,0:T(8,128)(2,1)S(1)}, u32[]{:S(2)}, u32[]{:S(2)}) async-start(bf16[8,16,4096]{2,1,0:T(8,128)(2,1)} %bitcast.14), calls=%async_computation.1 | async-start | bytes 2097152 | tf_op jit(solution)/shard_map/all_to_all | solution.py:96
  148.2 15.7 %all-to-all-done.1 = bf16[8,16,4096]{2,1,0:T(8,128)(2,1)S(1)} async-done(((bf16[8,16,4096]{2,1,0:T(8,128)(2,1)}), bf16[8,16,4096]{2,1,0:T(8,128)(2,1)S(1)}, u32[]{:S(2)}, u32[]{:S(2)}) %all-to-all-start.1) | async-done | bytes 1048608 | tf_op jit(solution)/shard_map/all_to_all | solution.py:96
  163.9 3.5 %multiply_reduce_fusion = bf16[128,4096]{1,0:T(8,128)(2,1)} fusion(bf16[8,16,4096]{2,1,0:T(8,128)(2,1)S(1)} %all-to-all-done.1, f32[8,128]{1,0:T(8,128)S(1)} %bitcast.81, s32[8,128]{1,0:T(8,128)S(1)} %copy.45, pred[8,128]{1,0:T(8,128)(4,1)S(1)} %bitcast.80), kind=kOutput, calls=%fused_computation | convolution fusion | flops 142114816 | bytes 2106368 | tf_op jit(solution)/shard_map/bcr,bcd->brd/dot_general | solution.py:97
  167.4 0.6 dynamic-slice
  168.7 83.0 %all-reduce.6.cloned.1.call-done = bf16[128,4096]{1,0:T(8,128)(2,1)} async-done(((bf16[128,4096]{1,0:T(8,128)(2,1)}), bf16[128,4096]{1,0:T(8,128)(2,1)}) %all-reduce.6.cloned.1.call-update) | async-done | bytes 1048592
  251.6 1.5 add_convert_fusion.1
  (32 shorter events, 0.7 us)
Async XLA Ops:
  6.5 103.5 %all-reduce.4.cloned.1.call-start = ((), (), s32[]{:S(2)}) async-start(), calls=%async_computation.2 | async-start | bytes 2097152 | tf_op jit(solution)/shard_map/psum | solution.py:67
  15.2 3.6 %copy-start = (bf16[512,4096]{1,0:T(8,128)(2,1)S(1)}, bf16[512,4096]{1,0:T(8,128)(2,1)}, u32[]{:S(2)}) copy-start(bf16[512,4096]{1,0:T(8,128)(2,1)} %param.21) | copy-start | bytes 12582916
  18.8 1.8 copy-start.3
  18.8 91.3 %copy-start.1 = (bf16[128,4096]{1,0:T(8,128)(2,1)S(1)}, bf16[128,4096]{1,0:T(8,128)(2,1)}, u32[]{:S(2)}) copy-start(bf16[128,4096]{1,0:T(8,128)(2,1)} %param.14) | copy-start | bytes 3145732
  18.8 93.0 %copy-start.2 = (f32[4096]{0:T(1024)S(1)}, f32[4096]{0:T(1024)}, u32[]{:S(2)}) copy-start(f32[4096]{0:T(1024)} %param.22) | copy-start | bytes 49156
  136.4 11.7 %copy-start.4 = (f32[128,8]{0,1:T(8,128)S(1)}, f32[128,8]{0,1:T(8,128)}, u32[]{:S(2)}) copy-start(f32[128,8]{0,1:T(8,128)} %param.24) | copy-start | bytes 12292
  144.5 19.4 %all-to-all-start.1 = ((bf16[8,16,4096]{2,1,0:T(8,128)(2,1)}), bf16[8,16,4096]{2,1,0:T(8,128)(2,1)S(1)}, u32[]{:S(2)}, u32[]{:S(2)}) async-start(bf16[8,16,4096]{2,1,0:T(8,128)(2,1)} %bitcast.14), calls=%async_computation.1 | async-start | bytes 2097152 | tf_op jit(solution)/shard_map/all_to_all | solution.py:96
  148.0 103.6 %all-reduce.6.cloned.1.call-start = ((), (), s32[]{:S(2)}) async-start(), calls=%async_computation.3 | async-start | bytes 2097152
  163.9 3.5 %copy-start.5 = (u32[128]{0:T(128)S(1)}, u32[128]{0:T(128)}, u32[]{:S(2)}) copy-start(u32[128]{0:T(128)} %constant.65) | copy-start | bytes 1540
Sparse Core Ops, SparseCore 0:
  20.7 89.3 all-reduce.3
  167.6 84.0 all-reduce.5
where the time goes:
time: 260 us
  waiting for transfers between devices  188 us (72%)
  matrix products  26 us (10%)
  blocking collectives  20.3 us (8%)
  between operations  14.2 us (5%)
  other arithmetic  5.8 us (2%)
  starting transfers between devices  3.6 us (1%)
    psum x1, waiting for transfers between devices, shards(): lax.psum(jnp.dot(heads_out, out_weight, preferred_element_type=jnp.float3...  89 us
    unnamed x3, waiting for transfers between devices  83 us
    all_to_all x1, blocking collectives, shards(): lax.all_to_all(outgoing, 'dp', split_axis=0, concat_axis=0, tiled=True)  20.3 us
    all_to_all x1, waiting for transfers between devices, shards(): lax.all_to_all(answered, 'dp', split_axis=0, concat_axis=0, tiled=True)  15.7 us
    dot_general x1, matrix products, shards(): jnp.dot(act, w_down[0], preferred_element_type=jnp.float32)  8.05 us
  transfers between devices with their start and end apart: 3, of which 3 were waited for; matrix products, arithmetic and copies ran while one was open for 0% of the time, Pallas kernels for 0%

commit v1 on v0

--- a/solution.py
+++ b/solution.py
@@ -64,9 +64,12 @@
     heads_out = attended.astype(jnp.bfloat16).reshape(row_count, head_count * head_size)
     share_rows = row_count // tensor_width
     first_own = column * share_rows
-    proj = lax.psum(
-        jnp.dot(heads_out, out_weight, preferred_element_type=jnp.float32).astype(jnp.bfloat16),
-        "tensor",
+    proj = jnp.sum(
+        lax.all_gather(
+            jnp.dot(heads_out, out_weight, preferred_element_type=jnp.float32).astype(jnp.bfloat16),
+            "tensor",
+        ),
+        axis=0,
     ).astype(jnp.float32)
     hidden_all = (residual_in.astype(jnp.float32) + proj).astype(jnp.bfloat16)
     normed = rms_normalize(hidden_all, norm_gain)

time: 260 us -> 293 us (1.13)
  waiting for transfers between devices: 188 us -> 213 us
  other arithmetic: 5.8 us -> 13.6 us
    all_gather x0 -> x1, waiting for transfers between devices: none -> 113 us  [shards(): lax.all_gather(jnp.dot(heads_out, out_weight, preferred_element_type=jnp....]
    psum x1 -> x0, waiting for transfers between devices: 89 us -> none  [shards(): lax.psum(jnp.dot(heads_out, out_weight, preferred_element_type=jnp.float3...]
    reduce_sum x0 -> x1, other arithmetic: none -> 8.99 us  [shards(): jnp.sum(lax.all_gather(jnp.dot(heads_out, out_weight, preferred_element_t...]
where the time goes in v1:
time: 293 us
  waiting for transfers between devices  213 us (73%)
  matrix products  26 us (9%)
  blocking collectives  20.3 us (7%)
  between operations  14.2 us (5%)
  other arithmetic  13.6 us (5%)
  starting transfers between devices  3.6 us (1%)
    all_gather x1, waiting for transfers between devices, shards(): lax.all_gather(jnp.dot(heads_out, out_weight, preferred_element_type=jnp....  113 us
    unnamed x3, waiting for transfers between devices  83.5 us
    all_to_all x1, blocking collectives, shards(): lax.all_to_all(outgoing, 'dp', split_axis=0, concat_axis=0, tiled=True)  20.3 us
    all_to_all x1, waiting for transfers between devices, shards(): lax.all_to_all(answered, 'dp', split_axis=0, concat_axis=0, tiled=True)  15.7 us
    reduce_sum x1, other arithmetic, shards(): jnp.sum(lax.all_gather(jnp.dot(heads_out, out_weight, preferred_element_t...  8.99 us
    dot_general x1, matrix products, shards(): jnp.dot(act, w_down[0], preferred_element_type=jnp.float32)  8.06 us
  transfers between devices with their start and end apart: 3, of which 3 were waited for; matrix products, arithmetic and copies ran while one was open for 0% of the time, Pallas kernels for 0%

profile of v1, /device:TPU:0, one launch (start us, length us, event | category | flops | bytes accessed | tf_op | source)
XLA Modules:
  0.0 292.6 jit_solution(5641972328492511167)
XLA Ops:
  6.5 1.1 dynamic-slice_convert_fusion
  7.6 0.9 reshape.50
  8.6 0.3 fusion.54
  8.9 0.8 iota_compare_fusion.1
  9.7 4.5 %fusion.65 = (f32[128,4]{1,0:T(8,128)S(1)}, f32[128,4,128]{2,1,0:T(4,128)S(1)}) fusion(bf16[128,4,128]{2,1,0:T(4,128)(2,1)S(1)} %reshape.50, bf16[128,1,128,128]{3,2,1,0:T(8,128)(2,1)} %param.18, pred[128,128]{1,0:T(8,128)(4,1)S(1)} %iota_compare_fusion.1), kind=kOutput, calls=%fused_computation.69 | convolution fusion | flops 16973312 | bytes 4605952 | tf_op jit(solution)/shard_map/rhd,rpd->rhp/dot_general | solution.py:42
  14.3 0.1 copy.40
  14.4 0.4 fusion.45
  14.9 0.1 copy.42
  15.2 3.6 %fusion.31 = bf16[128,4,128]{2,1,0:T(4,128)(2,1)S(1)} fusion(bf16[128,1,128,128]{3,2,1,0:T(8,128)(2,1)} %param.19, f32[128,4,128]{2,1,0:T(4,128)S(1)} %get-tuple-element.10, f32[128,128]{1,0:T(8,128)S(1)} %bitcast.79, f32[128,4]{1,0:T(8,128)S(1)} %copy.43, f32[128,4]{1,0:T(8,128)S(1)} %copy.42, f32[128,4]{1,0:T(8,128)S(1)} %copy.40), kind=kOutput, calls=%fused_computation.25 | convolution fusion | flops 17170432 | bytes 4659200 | tf_op jit(solution)/shard_map/rhp,rpd->rhd/dot_general | solution.py:59
  18.8 1.7 convolution_convert_fusion.1
  20.7 0.2 reduce_window_sum.11
  21.0 113.4 %all-gather.3.cloned.1.call-done = bf16[2048,4096]{1,0:T(8,128)(2,1)} async-done(((bf16[128,4096]{1,0:T(8,128)(2,1)}), bf16[2048,4096]{1,0:T(8,128)(2,1)}) %all-gather.3.cloned.1.call-update) | async-done | bytes 16777232 | tf_op jit(solution)/shard_map/all_gather | solution.py:68
  134.3 9.0 %reduce_sum.58 = bf16[128,4096]{1,0:T(8,128)(2,1)S(1)} reduce(bf16[16,128,4096]{2,1,0:T(8,128)(2,1)} %bitcast.75, bf16[]{:T(256)} %constant.52.clone.1), dimensions={0}, to_apply=%region_2.3 | reduce | flops 7864320 | bytes 17825794 | tf_op jit(solution)/shard_map/reduce_sum | solution.py:67
  143.3 0.5 fusion.13
  143.8 0.5 convolution_convert_fusion
  144.4 20.3 %all_to_all.10 = bf16[8,16,4096]{2,1,0:T(8,128)(2,1)S(1)} all-to-all(bf16[8,16,4096]{2,1,0:T(8,128)(2,1)S(1)} %convolution_convert_fusion), channel_id=1, replica_groups=mesh['dp'=8,'tensor'=16] {'dp'}, dimensions={0} | all-to-all | bytes 2097152 | tf_op jit(solution)/shard_map/all_to_all | solution.py:92
  164.7 3.8 %fusion.4 = f32[128,768]{1,0:T(8,128)S(1)} fusion(bf16[128,4096]{1,0:T(8,128)(2,1)S(1)} %bitcast.76, bf16[1,4096,768]{2,1,0:T(8,128)(2,1)} %param.25), kind=kOutput, calls=%fused_computation.5 | convolution fusion | flops 805306368 | bytes 7733248 | tf_op jit(solution)/shard_map/dot_general | solution.py:94
  168.5 8.1 %fusion.6 = bf16[128,4096]{1,0:T(8,128)(2,1)} fusion(bf16[1,768,4096]{2,1,0:T(8,128)(2,1)} %param.27, bf16[128,4096]{1,0:T(8,128)(2,1)S(1)} %bitcast.77, bf16[1,4096,768]{2,1,0:T(8,128)(2,1)} %param.26, f32[128,768]{1,0:T(8,128)S(1)} %fusion.4), kind=kOutput, calls=%fused_computation.7 | convolution fusion | flops 1611726848 | bytes 15073280 | tf_op jit(solution)/shard_map/dot_general | solution.py:97
  176.5 3.6 %all-to-all-start.1 = ((bf16[8,16,4096]{2,1,0:T(8,128)(2,1)}), bf16[8,16,4096]{2,1,0:T(8,128)(2,1)S(1)}, u32[]{:S(2)}, u32[]{:S(2)}) async-start(bf16[8,16,4096]{2,1,0:T(8,128)(2,1)} %bitcast.15), calls=%async_computation.1 | async-start | bytes 2097152 | tf_op jit(solution)/shard_map/all_to_all | solution.py:99
  180.3 15.7 %all-to-all-done.1 = bf16[8,16,4096]{2,1,0:T(8,128)(2,1)S(1)} async-done(((bf16[8,16,4096]{2,1,0:T(8,128)(2,1)}), bf16[8,16,4096]{2,1,0:T(8,128)(2,1)S(1)}, u32[]{:S(2)}, u32[]{:S(2)}) %all-to-all-start.1) | async-done | bytes 1048608 | tf_op jit(solution)/shard_map/all_to_all | solution.py:99
  196.0 3.5 %multiply_reduce_fusion = bf16[128,4096]{1,0:T(8,128)(2,1)} fusion(bf16[8,16,4096]{2,1,0:T(8,128)(2,1)S(1)} %all-to-all-done.1, f32[8,128]{1,0:T(8,128)S(1)} %bitcast.83, s32[8,128]{1,0:T(8,128)S(1)} %copy.45, pred[8,128]{1,0:T(8,128)(4,1)S(1)} %bitcast.82), kind=kOutput, calls=%fused_computation | convolution fusion | flops 142114816 | bytes 2106368 | tf_op jit(solution)/shard_map/bcr,bcd->brd/dot_general | solution.py:100
  199.5 0.6 dynamic-slice
  200.8 83.5 %all-reduce.3.cloned.1.call-done = bf16[128,4096]{1,0:T(8,128)(2,1)} async-done(((bf16[128,4096]{1,0:T(8,128)(2,1)}), bf16[128,4096]{1,0:T(8,128)(2,1)}) %all-reduce.3.cloned.1.call-update) | async-done | bytes 1048592
  284.3 1.5 add_convert_fusion.1
  (33 shorter events, 0.8 us)
Async XLA Ops:
  6.5 127.8 %all-gather.3.cloned.1.call-start = ((), (), s32[]{:S(2)}) async-start(), calls=%async_computation.2 | async-start | bytes 17825792 | tf_op jit(solution)/shard_map/all_gather | solution.py:68
  15.2 3.6 %copy-start = (bf16[512,4096]{1,0:T(8,128)(2,1)S(1)}, bf16[512,4096]{1,0:T(8,128)(2,1)}, u32[]{:S(2)}) copy-start(bf16[512,4096]{1,0:T(8,128)(2,1)} %param.21) | copy-start | bytes 12582916
  18.8 1.8 copy-start.3
  134.3 9.0 %copy-start.1 = (bf16[128,4096]{1,0:T(8,128)(2,1)S(1)}, bf16[128,4096]{1,0:T(8,128)(2,1)}, u32[]{:S(2)}) copy-start(bf16[128,4096]{1,0:T(8,128)(2,1)} %param.14) | copy-start | bytes 3145732
  134.3 9.5 %copy-start.2 = (f32[4096]{0:T(1024)S(1)}, f32[4096]{0:T(1024)}, u32[]{:S(2)}) copy-start(f32[4096]{0:T(1024)} %param.22) | copy-start | bytes 49156
  168.5 11.7 %copy-start.4 = (f32[128,8]{0,1:T(8,128)S(1)}, f32[128,8]{0,1:T(8,128)}, u32[]{:S(2)}) copy-start(f32[128,8]{0,1:T(8,128)} %param.24) | copy-start | bytes 12292
  176.5 19.4 %all-to-all-start.1 = ((bf16[8,16,4096]{2,1,0:T(8,128)(2,1)}), bf16[8,16,4096]{2,1,0:T(8,128)(2,1)S(1)}, u32[]{:S(2)}, u32[]{:S(2)}) async-start(bf16[8,16,4096]{2,1,0:T(8,128)(2,1)} %bitcast.15), calls=%async_computation.1 | async-start | bytes 2097152 | tf_op jit(solution)/shard_map/all_to_all | solution.py:99
  180.1 104.2 %all-reduce.3.cloned.1.call-start = ((), (), s32[]{:S(2)}) async-start(), calls=%async_computation.3 | async-start | bytes 2097152
  196.0 3.5 %copy-start.5 = (u32[128]{0:T(128)S(1)}, u32[128]{0:T(128)}, u32[]{:S(2)}) copy-start(u32[128]{0:T(128)} %constant.67) | copy-start | bytes 1540
Sparse Core Ops, SparseCore 0:
  20.6 113.6 all-gather.2
  199.6 84.5 all-reduce.2
